TPU v7x, 32 devices: a whole 2x2x4 slice. The times are simulated.
32 devices in a mesh: dp: 4 (over y, core), ctx: 2 (over x), tensor: 4 (over z).
Axes of the slice: x: 2, y: 2, z: 4, core: 2. Of those that a mesh axis runs over, the one named last changes fastest.
Arguments:
- layer_input: bfloat16 [4, 512, 8192], P('dp', ('ctx', 'tensor')), may hold values from -6 to 6
- queries: bfloat16 [4, 512, 8192], P('dp', 'ctx', 'tensor'), may hold values from -12 to 12
- forward_output: bfloat16 [4, 512, 8192], P('dp', 'ctx', 'tensor'), may hold values from -6 to 6
- attention_output_gradient: bfloat16 [4, 512, 8192], P('dp', 'ctx', 'tensor'), may hold values from -6 to 6
- key_weight: bfloat16 [8192, 1024], P(None, 'tensor'), may hold values from -3 to 3
- value_projection_weight: bfloat16 [8192, 1024], P(None, 'tensor'), may hold values from -0.0625 to 0.0625
- segment: int32 [4, 512], P('dp'), may hold values from 0 to 4, as said below
- block_table: int32 [4, 4, 4], P('dp'), may hold values from 0 to 1, as said below
- block_owner: int32 [4, 4], P('dp'), may hold values from 0 to 3, each once within a row
Outputs:
- query_grad: bfloat16 [4, 512, 8192], P('dp', 'ctx', 'tensor')
- input_grad: bfloat16 [4, 512, 8192], P('dp', ('ctx', 'tensor'))
- key_weight_grad: bfloat16 [8192, 1024], P(('dp', 'ctx'), 'tensor')
- value_weight_grad: bfloat16 [8192, 1024], P(('dp', 'ctx'), 'tensor')
Inputs may be any that keep to these rules, and one draw needn't show every extreme that they name: Along the logical positions of a group the segment never falls; the prompt (0) comes first and every rollout 1 to 4 is present. block_table[g, b, c] is 1 only where some position of logical block b may read some position of logical block c under the causal and segment rule; block_table[g, b, b] is 1 for every block; other such pairs may be 0. `block_owner`: each group's row holds every logical block once.
All inputs are finite; a program needn't handle non-finite values.
Results may differ from a plain program's by a relative error of at most 0.005.
The roundings to bfloat16 on the way count: a program that leaves them out, or rounds other values in their place, can miss the bound.
Values may be sent and summed in bfloat16 or wider, within the bound.
A program may use at most 128 MiB of HBM per device.

v0:
```python
import math
import jax
import jax.numpy as jnp
from jax import lax
from jax.sharding import PartitionSpec as P

HEAD_SIZE = 128
BLK = 128


def per_device(
    layer_input,
    queries,
    forward_output,
    attention_output_gradient,
    key_weight,
    value_projection_weight,
    segment,
    block_table,
    block_owner,
):
    softmax_scale = 1.0 / math.sqrt(HEAD_SIZE)
    local_rows = queries.shape[1]
    kv_local = key_weight.shape[1] // HEAD_SIZE
    q_local = queries.shape[2] // HEAD_SIZE
    queries_per_group = q_local // kv_local
    kv_width = kv_local * HEAD_SIZE
    gathered = lax.all_gather(layer_input, "tensor", axis=1, tiled=True)[0]
    projected_keys = jnp.dot(gathered, key_weight, preferred_element_type=jnp.float32)
    projected_values = jnp.dot(
        gathered, value_projection_weight, preferred_element_type=jnp.float32
    )
    kv_rows = jnp.concatenate([projected_keys, projected_values], axis=1).astype(jnp.bfloat16)
    owner_row = block_owner[0]
    segments_row = segment[0]
    table_row = block_table[0]
    blocks_here = local_rows // BLK
    ctx_index = lax.axis_index("ctx")
    own_blocks = lax.dynamic_slice_in_dim(owner_row, ctx_index * blocks_here, blocks_here)
    offsets = jnp.arange(BLK, dtype=jnp.int32)
    query_pos = (own_blocks[:, None] * BLK + offsets[None, :]).reshape(-1)
    query_seg = jnp.take(segments_row, query_pos)
    own_table = jnp.take(table_row, own_blocks, axis=0)
    query_heads = queries[0].reshape(local_rows, kv_local, queries_per_group, HEAD_SIZE)
    grad_heads = attention_output_gradient[0].reshape(
        local_rows, kv_local, queries_per_group, HEAD_SIZE
    )
    saved_heads = forward_output[0].reshape(local_rows, kv_local, queries_per_group, HEAD_SIZE)
    correction = jnp.sum(grad_heads.astype(jnp.float32) * saved_heads.astype(jnp.float32), axis=-1)
    correction = correction.transpose(1, 2, 0)

    def allowed_for(leading_row, row_count):
        key_blocks = lax.dynamic_slice_in_dim(owner_row, leading_row // BLK, row_count // BLK)
        key_pos = (key_blocks[:, None] * BLK + offsets[None, :]).reshape(-1)
        key_seg = jnp.take(segments_row, key_pos)
        table_part = jnp.take(own_table, key_blocks, axis=1) == 1
        table_full = jnp.broadcast_to(
            table_part[:, None, :, None], (blocks_here, BLK, row_count // BLK, BLK)
        )
        table_full = table_full.reshape(local_rows, row_count)
        same_tree = (key_seg[None, :] == 0) | (key_seg[None, :] == query_seg[:, None])
        return table_full & (key_pos[None, :] <= query_pos[:, None]) & same_tree

    def block_scores(block_rows, leading_row):
        row_count = block_rows.shape[0]
        block_keys = block_rows[:, :kv_width].reshape(row_count, kv_local, HEAD_SIZE)
        block_values = block_rows[:, kv_width:].reshape(row_count, kv_local, HEAD_SIZE)
        raw_scores = (
            jnp.einsum(
                "qhgd,khd->hgqk", query_heads, block_keys, preferred_element_type=jnp.float32
            )
            * softmax_scale
        )
        allowed = allowed_for(leading_row, row_count)
        return (jnp.where(allowed[None, None], raw_scores, -jnp.inf), block_keys, block_values)

    def stats_block(carried, block_rows, leading_row):
        running_max, running_sum = carried
        scores = block_scores(block_rows, leading_row)[0]
        new_max = jnp.maximum(running_max, jnp.max(scores, axis=-1))
        running_sum = running_sum * jnp.exp(running_max - new_max) + jnp.sum(
            jnp.exp(scores - new_max[..., None]), axis=-1
        )
        return (new_max, running_sum)

    def grads_block(carried, block_rows, leading_row, log_norm):
        query_sum, keyval_sum = carried
        row_count = block_rows.shape[0]
        scores, block_keys, block_values = block_scores(block_rows, leading_row)
        probabilities = jnp.exp(scores - log_norm[..., None])
        probs_low = probabilities.astype(jnp.bfloat16)
        value_gradient_rows = jnp.einsum(
            "hgqk,qhgd->khd", probs_low, grad_heads, preferred_element_type=jnp.float32
        )
        prob_grads = jnp.einsum(
            "qhgd,khd->hgqk", grad_heads, block_values, preferred_element_type=jnp.float32
        )
        score_low = (probabilities * (prob_grads - correction[..., None])).astype(jnp.bfloat16)
        query_sum = query_sum + jnp.einsum(
            "hgqk,khd->qhgd", score_low, block_keys, preferred_element_type=jnp.float32
        )
        key_gradient_rows = (
            jnp.einsum("hgqk,qhgd->khd", score_low, query_heads, preferred_element_type=jnp.float32)
            * softmax_scale
        )
        update = jnp.concatenate(
            [
                key_gradient_rows.reshape(row_count, kv_width),
                value_gradient_rows.reshape(row_count, kv_width),
            ],
            axis=1,
        )
        keyval_sum = lax.dynamic_update_slice_in_dim(keyval_sum, update, leading_row, 0)
        return (query_sum, keyval_sum)

    def over_blocks(block_step, carried, shard_part):
        row_count = shard_part.shape[0]
        block_size = math.gcd(row_count, max(512, local_rows))
        block_count = row_count // block_size
        pieces = shard_part.reshape(block_count, block_size, shard_part.shape[1])
        starts = block_size * jnp.arange(block_count, dtype=jnp.int32)

        def one_block(state_in, scan_item):
            block_rows, block_start = scan_item
            result = block_step(state_in, block_rows, block_start)
            return (result, None)

        carried, _ = lax.scan(one_block, carried, (pieces, starts))
        return carried

    stats_init = (
        jnp.full((kv_local, queries_per_group, local_rows), -1e30, jnp.float32),
        jnp.zeros((kv_local, queries_per_group, local_rows), jnp.float32),
    )
    seq_rows = local_rows * lax.axis_size("ctx")
    grads_init = (
        jnp.zeros((local_rows, kv_local, queries_per_group, HEAD_SIZE), jnp.float32),
        jnp.zeros((seq_rows, 2 * kv_width), jnp.float32),
    )
    running_max, running_sum = over_blocks(
        stats_block, stats_init, lax.all_gather(kv_rows, "ctx", axis=0, tiled=True)
    )
    log_norm = running_max + jnp.log(running_sum)

    def grads_fold(carried, shard_part):
        return over_blocks(
            lambda state, rows_in, start_in: grads_block(state, rows_in, start_in, log_norm),
            carried,
            shard_part,
        )

    query_sum, keyval_sum = grads_fold(
        grads_init, lax.all_gather(kv_rows, "ctx", axis=0, tiled=True)
    )
    own_grads = lax.psum_scatter(keyval_sum, "ctx", scatter_dimension=0, tiled=True).astype(
        jnp.bfloat16
    )
    query_grad = (
        (query_sum * softmax_scale).astype(jnp.bfloat16).reshape(1, local_rows, q_local * HEAD_SIZE)
    )
    term = lax.dot_general(
        own_grads[:, :kv_width],
        key_weight,
        (((1,), (1,)), ((), ())),
        preferred_element_type=jnp.float32,
    )
    input_grad = lax.psum_scatter(
        term
        + lax.dot_general(
            own_grads[:, kv_width:],
            value_projection_weight,
            (((1,), (1,)), ((), ())),
            preferred_element_type=jnp.float32,
        ),
        "tensor",
        scatter_dimension=0,
        tiled=True,
    )
    input_grad = input_grad.astype(jnp.bfloat16)[None]
    weight_sum = lax.psum_scatter(
        lax.dot_general(
            gathered, own_grads, (((0,), (0,)), ((), ())), preferred_element_type=jnp.float32
        ),
        ("dp", "ctx"),
        scatter_dimension=0,
        tiled=True,
    )
    key_weight_grad = weight_sum[:, :kv_width].astype(jnp.bfloat16)
    value_weight_grad = weight_sum[:, kv_width:].astype(jnp.bfloat16)
    return (query_grad, input_grad, key_weight_grad, value_weight_grad)


def solution(mesh):
    in_specs = (
        P("dp", ("ctx", "tensor"), None),
        P("dp", "ctx", "tensor"),
        P("dp", "ctx", "tensor"),
        P("dp", "ctx", "tensor"),
        P(None, "tensor"),
        P(None, "tensor"),
        P("dp", None),
        P("dp", None, None),
        P("dp", None),
    )
    out_specs = (
        P("dp", "ctx", "tensor"),
        P("dp", ("ctx", "tensor"), None),
        P(("dp", "ctx"), "tensor"),
        P(("dp", "ctx"), "tensor"),
    )
    return jax.shard_map(
        per_device, mesh=mesh, in_specs=in_specs, out_specs=out_specs, check_vma=False
    )
```

profile of v0, /device:TPU:0, one launch (start us, length us, event | category | flops | bytes accessed | tf_op | source)
XLA Modules:
  0.0 426.8 jit_solution(8074572103710751653)
XLA Ops:
  7.2 0.0 copy-start
  7.2 0.0 copy-start.10
  7.2 0.0 all-gather.2.cloned.1.call-start
  7.3 0.7 all-gather.2.cloned.1.call-update
  7.9 0.0 reduce-scatter.4.cloned.1.call-start
  8.0 0.7 bitcast_multiply_fusion.1
  8.7 0.1 compare_select_fusion.1
  8.7 3.5 gather_fusion.3
  12.3 0.8 bitcast_multiply_fusion
  13.1 0.1 fusion.26
  13.2 1.9 gather_fusion.1
  15.2 0.1 fusion.23
  15.2 0.6 gather_fusion
  15.8 0.1 compare_and_fusion.1
  15.9 0.1 broadcast_select_fusion
  16.0 0.1 copy.41
  16.1 0.6 gather_fusion.2
  16.6 0.1 bitcast_compare_fusion
  16.7 0.1 copy.42
  16.8 0.1 add_bitcast_fusion
  16.9 0.1 and_select_fusion.1
  17.0 0.1 broadcast_compare_fusion
  17.0 0.1 broadcast_in_dim.108
  17.2 0.2 fusion.19
  17.4 0.3 copy.43
  17.7 0.5 copy.69
  18.2 1.5 copy.71
  19.8 1.6 copy.53
  21.4 0.2 convert_bitcast_fusion
  21.6 0.4 copy.72
  22.0 0.9 multiply_reduce_fusion
  22.9 0.1 copy.48
  23.0 70.1 %all-gather.2.cloned.1.call-done = bf16[1,256,8192]{2,1,0:T(8,128)(2,1)} async-done(((bf16[1,64,8192]{2,1,0:T(8,128)(2,1)}), bf16[1,256,8192]{2,1,0:T(8,128)(2,1)}) %all-gather.2.cloned.1.call-update) | async-done | bytes 4194320 | tf_op jit(solution)/shard_map/all_gather | solution.py:28
  93.1 5.3 %fusion.16 = bf16[256,256]{0,1:T(8,128)(2,1)S(1)} fusion(bf16[8192,256]{1,0:T(8,128)(2,1)} %param.18, bf16[1,256,8192]{2,1,0:T(8,128)(2,1)} %all-gather.2.cloned.1.call-done), kind=kOutput, calls=%fused_computation.27 | convolution fusion | flops 1073807360 | bytes 8519680 | tf_op jit(solution)/shard_map/dot_general | solution.py:30
  98.5 0.6 copy-done.3
  99.0 1.9 fusion.13
  100.9 8.9 %all_gather.8 = bf16[512,512]{0,1:T(8,128)(2,1)S(1)} all-gather(bf16[256,512]{0,1:T(8,128)(2,1)S(1)} %pad_maximum_fusion.1), channel_id=1, replica_groups=mesh['dp'=4,'ctx'=2,'tensor'=4] {'ctx'}, dimensions={0}, use_global_device_ids=true | all-gather | bytes 786432 | tf_op jit(solution)/shard_map/all_gather | solution.py:153
  109.9 1.4 fusion.3
  111.3 0.0 copy-start.8
  111.3 1.7 exponential_reduce_fusion
  113.0 2.3 fusion.9
  115.4 2.9 fusion.1
  118.2 2.0 copy-done.5
  120.2 1.5 fusion.12
  121.7 1.0 pad_maximum_fusion
  122.7 0.0 reduce-scatter.4.cloned.1.call-update
  122.7 0.0 reduce-scatter.6.cloned.1.call-start
  122.8 19.1 %reduce-scatter.4.cloned.1.call-done = f32[256,512]{0,1:T(8,128)} async-done(((f32[512,512]{0,1:T(8,128)}), f32[256,512]{0,1:T(8,128)}) %reduce-scatter.4.cloned.1.call-update) | async-done | bytes 524304 | tf_op jit(solution)/shard_map/reduce_scatter | solution.py:155
  141.9 1.1 convert_element_type.47
  143.0 3.6 fusion.21
  146.6 4.5 %convolution_add_fusion = f32[256,8192]{1,0:T(8,128)} fusion(f32[256,8192]{1,0:T(8,128)S(1)} %fusion.21, bf16[8192,256]{1,0:T(8,128)(2,1)S(1)} %copy-done.4, bf16[256,512]{0,1:T(8,128)(2,1)S(1)} %convert_element_type.47), kind=kOutput, calls=%fused_computation.5 | convolution fusion | flops 1075838976 | bytes 21102592 | tf_op jit(solution)/shard_map/dot_general | solution.py:169
  151.2 0.0 reduce-scatter.6.cloned.1.call-update
  151.2 0.3 reduce-scatter.8.cloned.1.call-start
  151.5 10.9 %convolution_bitcast_fusion = f32[8192,512]{0,1:T(8,128)} fusion(bf16[256,512]{0,1:T(8,128)(2,1)S(1)} %convert_element_type.47, bf16[1,256,8192]{2,1,0:T(8,128)(2,1)} %all-gather.2.cloned.1.call-done), kind=kOutput, calls=%fused_computation.4 | convolution fusion | flops 2147483648 | bytes 21233664 | tf_op jit(solution)/shard_map/dot_general | solution.py:181
  162.4 0.0 reduce-scatter.8.cloned.1.call-update
  162.4 2.9 multiply_convert_fusion
  165.3 1.4 copy.54
  166.7 129.1 %reduce-scatter.6.cloned.1.call-done = f32[64,8192]{1,0:T(8,128)} async-done(((f32[256,8192]{1,0:T(8,128)}), f32[64,8192]{1,0:T(8,128)}) %reduce-scatter.6.cloned.1.call-update) | async-done | bytes 2097168 | tf_op jit(solution)/shard_map/reduce_scatter | solution.py:167
  295.8 2.7 convert_bitcast_fusion.1
  298.5 117.9 %reduce-scatter.8.cloned.1.call-done = f32[1024,512]{0,1:T(8,128)} async-done(((f32[8192,512]{0,1:T(8,128)}), f32[1024,512]{0,1:T(8,128)}) %reduce-scatter.8.cloned.1.call-update) | async-done | bytes 2097168 | tf_op jit(solution)/shard_map/reduce_scatter | solution.py:180
  416.4 1.7 convert.13
  418.1 0.1 fusion.27
  418.2 1.0 copy.56
  419.2 1.0 copy.55
  (27 shorter events, 0.2 us)
Async XLA Ops:
  7.2 1.6 copy-start
  7.2 8.0 %copy-start.10 = (s32[1,4]{1,0:T(1,128)S(1)}, s32[1,4]{1,0:T(1,128)}, u32[]{:S(2)}) copy-start(s32[1,4]{1,0:T(1,128)} %param.21) | copy-start | bytes 52
  7.2 8.1 %copy-start.9 = (s32[1,4,4]{2,1,0:T(4,128)S(1)}, s32[1,4,4]{2,1,0:T(4,128)}, u32[]{:S(2)}) copy-start(s32[1,4,4]{2,1,0:T(4,128)} %param.20) | copy-start | bytes 196
  7.2 10.5 %copy-start.7 = (bf16[1,256,2048]{2,1,0:T(8,128)(2,1)S(1)}, bf16[1,256,2048]{2,1,0:T(8,128)(2,1)}, u32[]{:S(2)}) copy-start(bf16[1,256,2048]{2,1,0:T(8,128)(2,1)} %param.14) | copy-start | bytes 3145732
  7.2 85.9 %all-gather.2.cloned.1.call-start = ((), (), s32[]{:S(2)}) async-start(), calls=%async_computation.3 | async-start | bytes 5242880 | tf_op jit(solution)/shard_map/all_gather | solution.py:28
  7.9 133.9 %reduce-scatter.4.cloned.1.call-start = ((), (), s32[]{:S(2)}) async-start(), calls=%async_computation.4 | async-start | bytes 1572864 | tf_op jit(solution)/shard_map/reduce_scatter | solution.py:155
  12.3 9.1 %copy-start.6 = (bf16[1,256,2048]{2,1,0:T(8,128)(2,1)S(1)}, bf16[1,256,2048]{2,1,0:T(8,128)(2,1)}, u32[]{:S(2)}) copy-start(bf16[1,256,2048]{2,1,0:T(8,128)(2,1)} %param.15) | copy-start | bytes 3145732
  93.1 5.3 %copy-start.2 = (bf16[1,256,8192]{2,1,0:T(8,128)(2,1)S(1)}, bf16[1,256,8192]{2,1,0:T(8,128)(2,1)}, u32[]{:S(2)}) copy-start(bf16[1,256,8192]{2,1,0:T(8,128)(2,1)} %all-gather.2.cloned.1.call-done) | copy-start | bytes 12582916
  93.1 5.9 %copy-start.3 = (bf16[8192,256]{1,0:T(8,128)(2,1)S(1)}, bf16[8192,256]{1,0:T(8,128)(2,1)}, u32[]{:S(2)}) copy-start(bf16[8192,256]{1,0:T(8,128)(2,1)} %param.17) | copy-start | bytes 12582916
  111.3 1.8 copy-start.8
  118.2 2.0 copy-start.5
  122.7 173.1 %reduce-scatter.6.cloned.1.call-start = ((), (), s32[]{:S(2)}) async-start(), calls=%async_computation.5 | async-start | bytes 10485760 | tf_op jit(solution)/shard_map/reduce_scatter | solution.py:167
  143.0 3.7 copy-start.4
  151.2 265.2 %reduce-scatter.8.cloned.1.call-start = ((), (), s32[]{:S(2)}) async-start(), calls=%async_computation.6 | async-start | bytes 18874368 | tf_op jit(solution)/shard_map/reduce_scatter | solution.py:180
  295.8 124.4 %copy-start.1 = (s32[1,512]{1,0:T(1,128)S(1)}, s32[1,512]{1,0:T(1,128)}, u32[]{:S(2)}) copy-start(s32[1,512]{1,0:T(1,128)} %param.19) | copy-start | bytes 6148
Sparse Core Ops, SparseCore 0:
  9.6 83.4 all-gather.1
  122.9 18.9 reduce-scatter.3
  151.3 144.4 reduce-scatter.5
  299.7 116.6 reduce-scatter.7
where the time goes:
time: 427 us
  waiting for transfers between devices  337 us (79%)
  matrix products  37.2 us (9%)
  local copies, waits for them, and re-layouts  17.4 us (4%)
  between operations  14.1 us (3%)
  other arithmetic  11.9 us (3%)
  blocking collectives  8.91 us (2%)
    reduce_scatter x1, waiting for transfers between devices, per_device(): lax.psum_scatter(term + lax.dot_general(own_grads[:, kv_width:], value_pr...  129 us
    reduce_scatter x1, waiting for transfers between devices, per_device(): lax.psum_scatter(lax.dot_general(gathered, own_grads, (((0,), (0,)), ((),...  118 us
    all_gather x1, waiting for transfers between devices, per_device(): gathered = lax.all_gather(layer_input, 'tensor', axis=1, tiled=True)[0]  70.1 us
    reduce_scatter x1, waiting for transfers between devices, per_device(): lax.psum_scatter(keyval_sum, 'ctx', scatter_dimension=0, tiled=True)  19.1 us
    dot_general x1, matrix products, per_device(): lax.dot_general(gathered, own_grads, (((0,), (0,)), ((), ())), preferred_...  10.9 us
    all_gather x1, blocking collectives, per_device(): lax.all_gather(kv_rows, 'ctx', axis=0, tiled=True)  8.91 us
  transfers between devices with their start and end apart: 4, of which 4 were waited for; matrix products, arithmetic and copies ran while one was open for 8% of the time, Pallas kernels for 0%

commit v1 on v0

--- a/solution.py
+++ b/solution.py
@@ -6,6 +6,11 @@
 
 HEAD_SIZE = 128
 BLK = 128
+
+
+def all_by_exchange(block, mesh_axis, along):
+    sent = jnp.stack([block] * lax.axis_size(mesh_axis))
+    return jnp.concatenate(lax.all_to_all(sent, mesh_axis, 0, 0), axis=along)
 
 
 def per_device(
@@ -149,9 +154,7 @@
             shard_part,
         )
 
-    query_sum, keyval_sum = grads_fold(
-        grads_init, lax.all_gather(kv_rows, "ctx", axis=0, tiled=True)
-    )
+    query_sum, keyval_sum = grads_fold(grads_init, all_by_exchange(kv_rows, "ctx", 0))
     own_grads = lax.psum_scatter(keyval_sum, "ctx", scatter_dimension=0, tiled=True).astype(
         jnp.bfloat16
     )

time: 427 us -> 435 us (1.019)
  transfers between devices with their start and end apart: 4 -> 5, of which waited for: 4 -> 5; matrix products, arithmetic and copies ran while one was open for 8% -> 8% of each run, Pallas kernels for 0% -> 0%
where the time goes in v1:
time: 435 us
  waiting for transfers between devices  340 us (78%)
  matrix products  38.5 us (9%)
  local copies, waits for them, and re-layouts  16.5 us (4%)
  between operations  14.1 us (3%)
  other arithmetic  12.7 us (3%)
  blocking collectives  8.79 us (2%)
    reduce_scatter x1, waiting for transfers between devices, per_device(): lax.psum_scatter(term + lax.dot_general(own_grads[:, kv_width:], value_pr...  129 us
    reduce_scatter x1, waiting for transfers between devices, per_device(): lax.psum_scatter(lax.dot_general(gathered, own_grads, (((0,), (0,)), ((),...  118 us
    all_gather x1, waiting for transfers between devices, per_device(): gathered = lax.all_gather(layer_input, 'tensor', axis=1, tiled=True)[0]  70.2 us
    reduce_scatter x1, waiting for transfers between devices, per_device(): lax.psum_scatter(keyval_sum, 'ctx', scatter_dimension=0, tiled=True)  18.3 us
    dot_general x1, matrix products, per_device(): lax.dot_general(gathered, own_grads, (((0,), (0,)), ((), ())), preferred_...  10.9 us
    all_gather x1, blocking collectives, per_device(): lax.all_gather(kv_rows, 'ctx', axis=0, tiled=True)  8.79 us
  transfers between devices with their start and end apart: 5, of which 5 were waited for; matrix products, arithmetic and copies ran while one was open for 8% of the time, Pallas kernels for 0%

profile of v1, /device:TPU:0, one launch (start us, length us, event | category | flops | bytes accessed | tf_op | source)
XLA Modules:
  0.0 434.8 jit_solution(18108098522488902661)
XLA Ops:
  7.3 0.7 all-gather.2.cloned.1.call-update
  8.0 0.7 bitcast_multiply_fusion.1
  8.6 0.1 compare_select_fusion.1
  8.7 3.5 gather_fusion.3
  12.2 0.8 bitcast_multiply_fusion
  13.1 0.1 fusion.28
  13.1 1.9 gather_fusion.1
  15.1 0.1 fusion.25
  15.2 0.6 gather_fusion
  15.8 0.1 compare_and_fusion.1
  15.8 0.1 broadcast_select_fusion
  15.9 0.1 copy.49
  16.0 0.6 gather_fusion.2
  16.6 0.1 bitcast_compare_fusion
  16.7 0.1 copy.50
  16.8 0.1 add_bitcast_fusion
  16.8 0.1 and_select_fusion.1
  16.9 0.1 broadcast_compare_fusion
  17.0 0.1 broadcast_in_dim.108
  17.1 0.2 fusion.21
  17.4 0.3 copy.51
  17.7 0.5 copy.83
  18.2 1.5 copy.85
  19.8 1.6 copy.64
  21.3 0.2 convert_bitcast_fusion
  21.6 0.4 copy.86
  22.0 0.9 multiply_reduce_fusion
  22.9 0.1 copy.59
  23.0 70.2 %all-gather.2.cloned.1.call-done = bf16[1,256,8192]{2,1,0:T(8,128)(2,1)} async-done(((bf16[1,64,8192]{2,1,0:T(8,128)(2,1)}), bf16[1,256,8192]{2,1,0:T(8,128)(2,1)}) %all-gather.2.cloned.1.call-update) | async-done | bytes 4194320 | tf_op jit(solution)/shard_map/all_gather | solution.py:33
  93.2 5.3 %fusion.18 = bf16[256,256]{0,1:T(8,128)(2,1)S(1)} fusion(bf16[8192,256]{1,0:T(8,128)(2,1)} %param.18, bf16[1,256,8192]{2,1,0:T(8,128)(2,1)} %all-gather.2.cloned.1.call-done), kind=kOutput, calls=%fused_computation.29 | convolution fusion | flops 1073807360 | bytes 8519680 | tf_op jit(solution)/shard_map/dot_general | solution.py:35
  98.5 0.6 copy-done.3
  99.1 1.9 fusion.15
  101.0 8.8 %all_gather.7 = bf16[512,512]{0,1:T(8,128)(2,1)S(1)} all-gather(bf16[256,512]{0,1:T(8,128)(2,1)S(1)} %pad_maximum_fusion.1), channel_id=1, replica_groups=mesh['dp'=4,'ctx'=2,'tensor'=4] {'ctx'}, dimensions={0}, use_global_device_ids=true | all-gather | bytes 786432 | tf_op jit(solution)/shard_map/all_gather | solution.py:146
  109.8 0.8 maximum_maximum_fusion
  110.6 3.5 all-to-all-start
  114.1 0.2 reduce-scatter.4.cloned.1.call-start
  114.3 1.4 fusion.4
  115.7 1.7 exponential_reduce_fusion
  117.5 4.1 all-to-all-done
  121.6 0.2 copy.47
  121.8 0.1 copy.56
  122.0 0.1 copy.48
  122.1 1.3 fusion.31
  123.4 2.3 fusion.11
  125.7 2.9 fusion.1
  128.6 1.5 fusion.14
  130.1 0.5 copy-done.5
  130.6 1.0 pad_maximum_fusion
  131.6 0.0 reduce-scatter.6.cloned.1.call-start
  131.7 18.3 %reduce-scatter.4.cloned.1.call-done = f32[256,512]{0,1:T(8,128)} async-done(((f32[512,512]{0,1:T(8,128)}), f32[256,512]{0,1:T(8,128)}) %reduce-scatter.4.cloned.1.call-update) | async-done | bytes 524304 | tf_op jit(solution)/shard_map/reduce_scatter | solution.py:158
  150.0 1.1 convert_element_type.54
  151.0 3.6 fusion.23
  154.7 4.5 %convolution_add_fusion = f32[256,8192]{1,0:T(8,128)} fusion(f32[256,8192]{1,0:T(8,128)S(1)} %fusion.23, bf16[8192,256]{1,0:T(8,128)(2,1)S(1)} %copy-done.4, bf16[256,512]{0,1:T(8,128)(2,1)S(1)} %convert_element_type.54), kind=kOutput, calls=%fused_computation.5 | convolution fusion | flops 1075838976 | bytes 21102592 | tf_op jit(solution)/shard_map/dot_general | solution.py:172
  159.3 0.3 reduce-scatter.8.cloned.1.call-start
  159.5 10.9 %convolution_bitcast_fusion = f32[8192,512]{0,1:T(8,128)} fusion(bf16[256,512]{0,1:T(8,128)(2,1)S(1)} %convert_element_type.54, bf16[1,256,8192]{2,1,0:T(8,128)(2,1)} %all-gather.2.cloned.1.call-done), kind=kOutput, calls=%fused_computation.4 | convolution fusion | flops 2147483648 | bytes 21233664 | tf_op jit(solution)/shard_map/dot_general | solution.py:184
  170.5 2.9 multiply_convert_fusion
  173.4 1.4 copy.65
  174.8 129.1 %reduce-scatter.6.cloned.1.call-done = f32[64,8192]{1,0:T(8,128)} async-done(((f32[256,8192]{1,0:T(8,128)}), f32[64,8192]{1,0:T(8,128)}) %reduce-scatter.6.cloned.1.call-update) | async-done | bytes 2097168 | tf_op jit(solution)/shard_map/reduce_scatter | solution.py:170
  303.9 2.7 convert_bitcast_fusion.1
  306.6 117.9 %reduce-scatter.8.cloned.1.call-done = f32[1024,512]{0,1:T(8,128)} async-done(((f32[8192,512]{0,1:T(8,128)}), f32[1024,512]{0,1:T(8,128)}) %reduce-scatter.8.cloned.1.call-update) | async-done | bytes 2097168 | tf_op jit(solution)/shard_map/reduce_scatter | solution.py:183
  424.5 1.7 convert.17
  426.2 0.1 fusion.29
  426.3 1.0 copy.67
  427.3 1.0 copy.66
  (35 shorter events, 0.3 us)
Async XLA Ops:
  7.2 1.5 copy-start
  7.2 7.9 %copy-start.10 = (s32[1,4]{1,0:T(1,128)S(1)}, s32[1,4]{1,0:T(1,128)}, u32[]{:S(2)}) copy-start(s32[1,4]{1,0:T(1,128)} %param.21) | copy-start | bytes 52
  7.2 8.0 %copy-start.9 = (s32[1,4,4]{2,1,0:T(4,128)S(1)}, s32[1,4,4]{2,1,0:T(4,128)}, u32[]{:S(2)}) copy-start(s32[1,4,4]{2,1,0:T(4,128)} %param.20) | copy-start | bytes 196
  7.2 10.5 %copy-start.7 = (bf16[1,256,2048]{2,1,0:T(8,128)(2,1)S(1)}, bf16[1,256,2048]{2,1,0:T(8,128)(2,1)}, u32[]{:S(2)}) copy-start(bf16[1,256,2048]{2,1,0:T(8,128)(2,1)} %param.14) | copy-start | bytes 3145732
  7.2 86.0 %all-gather.2.cloned.1.call-start = ((), (), s32[]{:S(2)}) async-start(), calls=%async_computation.4 | async-start | bytes 5242880 | tf_op jit(solution)/shard_map/all_gather | solution.py:33
  12.2 9.1 %copy-start.6 = (bf16[1,256,2048]{2,1,0:T(8,128)(2,1)S(1)}, bf16[1,256,2048]{2,1,0:T(8,128)(2,1)}, u32[]{:S(2)}) copy-start(bf16[1,256,2048]{2,1,0:T(8,128)(2,1)} %param.15) | copy-start | bytes 3145732
  93.2 5.3 %copy-start.2 = (bf16[1,256,8192]{2,1,0:T(8,128)(2,1)S(1)}, bf16[1,256,8192]{2,1,0:T(8,128)(2,1)}, u32[]{:S(2)}) copy-start(bf16[1,256,8192]{2,1,0:T(8,128)(2,1)} %all-gather.2.cloned.1.call-done) | copy-start | bytes 12582916
  93.2 5.9 %copy-start.3 = (bf16[8192,256]{1,0:T(8,128)(2,1)S(1)}, bf16[8192,256]{1,0:T(8,128)(2,1)}, u32[]{:S(2)}) copy-start(bf16[8192,256]{1,0:T(8,128)(2,1)} %param.17) | copy-start | bytes 12582916
  110.6 10.9 %all-to-all-start = ((bf16[2,256,512]{1,2,0:T(8,128)(2,1)}), bf16[2,256,512]{1,2,0:T(8,128)(2,1)S(1)}, u32[]{:S(2)}, u32[]{:S(2)}) async-start(bf16[2,256,512]{1,2,0:T(8,128)(2,1)} %maximum_maximum_fusion), calls=%async_computation | async-start | bytes 1048576 | tf_op jit(solution)/shard_map/all_to_all | solution.py:13
  114.1 35.8 %reduce-scatter.4.cloned.1.call-start = ((), (), s32[]{:S(2)}) async-start(), calls=%async_computation.5 | async-start | bytes 1572864 | tf_op jit(solution)/shard_map/reduce_scatter | solution.py:158
  122.1 1.3 copy-start.8
  128.6 2.0 copy-start.5
  131.6 172.3 %reduce-scatter.6.cloned.1.call-start = ((), (), s32[]{:S(2)}) async-start(), calls=%async_computation.6 | async-start | bytes 10485760 | tf_op jit(solution)/shard_map/reduce_scatter | solution.py:170
  151.0 3.7 copy-start.4
  159.3 265.2 %reduce-scatter.8.cloned.1.call-start = ((), (), s32[]{:S(2)}) async-start(), calls=%async_computation.7 | async-start | bytes 18874368 | tf_op jit(solution)/shard_map/reduce_scatter | solution.py:183
  303.9 124.4 %copy-start.1 = (s32[1,512]{1,0:T(1,128)S(1)}, s32[1,512]{1,0:T(1,128)}, u32[]{:S(2)}) copy-start(s32[1,512]{1,0:T(1,128)} %param.19) | copy-start | bytes 6148
Sparse Core Ops, SparseCore 0:
  9.6 83.5 all-gather.1
  131.8 18.1 reduce-scatter.3
  159.4 144.4 reduce-scatter.5
  307.7 116.6 reduce-scatter.7
